TPU v7x, 128 devices: a whole 4x4x4 slice. The times are simulated.
128 devices in a mesh: tm: 4 (over x), op: 32 (over y, z, core).
Axes of the slice: x: 4, y: 4, z: 4, core: 2. Of those that a mesh axis runs over, the one named last changes fastest.
Arguments:
- sink_elem: bfloat16 [2, 4, 2048, 16384], P(None, 'tm', 'op'), may hold values from -6 to 6
- source_elem: bfloat16 [2, 2, 2048, 16384], P(None, None, None, 'op'), may hold values from -6 to 6
- peram: bfloat16 [2, 4, 2, 512, 512], P(None, 'tm', None, 'op'), may hold values from -4 to 4
- pair_list: int32 [16, 1], replicated, may hold values from 0 to 15
- spin_sets: int32 [16, 3], replicated, may hold values from 0 to 3
Outputs:
- correlator: float32 [2, 4, 2, 16, 1], P(None, 'tm')
All inputs are finite; a program needn't handle non-finite values.
Results may differ from a plain program's by a relative error of at most 0.0041.
Values may be sent and summed in bfloat16 or wider, within the bound.
A program may use at most 192 MiB of HBM per device.

v0:
```python
import jax
import jax.numpy as jnp
from jax import lax
from jax.sharding import PartitionSpec as P

NEV = 128
NSPIN = 4
NOP = 16
TSRC = 2
PAIRS = 1


def complex_matrix(block):
    upper = jnp.concatenate([block[0], block[1]], axis=1)
    lower = jnp.concatenate([-block[1], block[0]], axis=1)
    return jnp.stack([upper, lower])


def on_device(sink_elem, source_elem, peram, pair_list, spin_sets):
    tau_all = lax.all_gather(peram, "op", axis=3, tiled=True)
    position = lax.axis_index("op")
    rows = sink_elem.shape[2]
    local_times = sink_elem.shape[1]
    span = min(rows, NEV)
    cols = source_elem.shape[3]

    def spin_block(local, t0, left, right):
        return lax.dynamic_slice(tau_all[:, local, t0], (0, left * NEV, right * NEV), (2, NEV, NEV))

    def sink_side(local, t0, p):
        op_now = (position * rows + 0) // NEV
        mine = spin_sets[op_now]
        theirs = spin_sets[pair_list[op_now, p]]
        third = complex_matrix(spin_block(local, t0, mine[2], theirs[2]))
        second = complex_matrix(spin_block(local, t0, mine[1], theirs[1]))
        phi = sink_elem[:, local, 0:span].reshape(2, span * NEV, NEV)
        x_both = jnp.einsum("cxk,ckb->xb", phi, third, preferred_element_type=jnp.float32)
        x_both = x_both.astype(jnp.bfloat16).reshape(span, NEV, 2, NEV)
        y_both = jnp.einsum("ijck,cjb->ibk", x_both, second, preferred_element_type=jnp.float32)
        y_both = y_both.astype(jnp.bfloat16).reshape(span, 2, NEV * NEV)
        pieces = jnp.transpose(y_both, (1, 0, 2))
        return pieces

    partial_terms = {}
    combos = [
        (local, t0, p) for local in range(local_times) for t0 in range(TSRC) for p in range(PAIRS)
    ]
    stacked = jnp.stack([sink_side(local, t0, p) for local, t0, p in combos], axis=1)
    columns = lax.all_to_all(stacked, "op", split_axis=3, concat_axis=2, tiled=True)
    for index, combo in enumerate(combos):
        column_t0 = combo[1]
        other = pair_list[:, combo[2]]
        source = source_elem[:, column_t0].reshape(2, NOP, NEV, cols)
        chosen = jnp.take(source, other, axis=1)
        tiles = columns[:, index].reshape(2, NOP, NEV, cols)

        def inner(a, b):
            return jnp.einsum("oic,ojc->oij", a, b, preferred_element_type=jnp.float32)

        m_re = inner(tiles[0], chosen[0]) + inner(tiles[1], chosen[1])
        m_im = inner(tiles[1], chosen[0]) - inner(tiles[0], chosen[1])
        blocks = tau_all[:, combo[0], column_t0].reshape(2, NSPIN, NEV, NSPIN, NEV)
        blocks = jnp.transpose(blocks, (1, 3, 0, 2, 4))
        first = blocks[spin_sets[:, 0], spin_sets[other, 0]].astype(jnp.float32)
        c_re = jnp.sum(first[:, 0] * m_re - first[:, 1] * m_im, axis=(1, 2))
        c_im = jnp.sum(first[:, 0] * m_im + first[:, 1] * m_re, axis=(1, 2))
        partial_terms[combo] = jnp.stack([c_re, c_im])
    local = 0
    per_time = []
    for t0 in range(TSRC):
        per_time.append(jnp.stack([partial_terms[local, t0, 0]], axis=-1))
    per_local = [jnp.stack(per_time, axis=1)]
    partial_sum = jnp.stack(per_local, axis=1)
    totals = lax.psum(partial_sum, "op")
    return totals * (1.0 / float(NEV**3))


def solution(mesh):
    in_specs = (
        P(None, "tm", "op", None),
        P(None, None, None, "op"),
        P(None, "tm", None, "op", None),
        P(),
        P(),
    )
    out_specs = P(None, "tm", None, None, None)
    return jax.shard_map(
        on_device, mesh=mesh, in_specs=in_specs, out_specs=out_specs, check_vma=False
    )
```

profile of v0, /device:TPU:1, one launch (start us, length us, event | category | flops | bytes accessed | tf_op | source)
XLA Modules:
  0.0 462.1 jit_solution(5356037397111504323)
XLA Ops:
  6.5 1.5 copy.40
  15.2 7.4 %reshape_squeeze.19 = bf16[2,8192,128]{2,1,0:T(8,128)(2,1)} reshape(bf16[2,1,64,16384]{3,2,1,0:T(8,128)(2,1)} %param.7) | data formatting | bytes 8388608 | tf_op jit(solution)/shard_map/reshape;squeeze | solution.py:36
  22.6 34.7 %all-gather.2.cloned.1.call-done = bf16[2,1,2,512,512]{4,2,1,0,3:T(2,128)(2,1)} async-done(((bf16[2,1,2,16,512]{4,2,1,0,3:T(2,128)(2,1)}), bf16[2,1,2,512,512]{4,2,1,0,3:T(2,128)(2,1)}) %all-gather.2.cloned.1.call-update) | async-done | bytes 2097168 | tf_op jit(solution)/shard_map/all_gather | solution.py:20
  57.3 6.5 %fusion.57 = (bf16[2,1,1,512,512]{4,2,1,0,3:T(2,128)(2,1)}, bf16[2,1,1,512,512]{4,2,1,0,3:T(2,128)(2,1)S(1)}) fusion(bf16[2,1,2,512,512]{4,2,1,0,3:T(2,128)(2,1)} %all-gather.2.cloned.1.call-done), kind=kLoop, calls=%fused_computation.113 | loop fusion | bytes 4194304 | tf_op jit(solution)/shard_map/slice | solution.py:62
  63.8 4.6 copy.59
  68.4 4.2 copy.60
  74.2 3.5 fusion.15
  78.9 7.4 %fusion.2 = bf16[64,256,128]{2,1,0:T(8,128)(2,1)} fusion(bf16[64,128,2,128]{1,0,3,2:T(8,128)(2,1)S(1)} %bitcast.218, bf16[1,128,256]{1,2,0:T(8,128)(2,1)S(1)} %get-tuple-element.35, bf16[1,128,256]{1,2,0:T(8,128)(2,1)S(1)} %get-tuple-element.34), kind=kOutput, calls=%fused_computation.12 | convolution fusion | flops 1076101120 | bytes 8519680 | tf_op jit(solution)/shard_map/ijck,cjb->ibk/dot_general | solution.py:39
  86.4 6.9 %reshape.75 = bf16[64,2,16384]{2,1,0:T(2,128)(2,1)} reshape(bf16[64,256,128]{2,1,0:T(8,128)(2,1)} %fusion.2) | data formatting | bytes 8388608 | tf_op jit(solution)/shard_map/reshape | solution.py:40
  93.2 6.6 %copy.83 = bf16[64,2,16384]{2,0,1:T(8,128)(2,1)} copy(bf16[64,2,16384]{2,1,0:T(2,128)(2,1)} %reshape.75) | data formatting | bytes 8388608 | tf_op jit(solution)/shard_map/reshape | solution.py:40
  102.4 7.4 %fusion.3 = bf16[64,256,128]{2,1,0:T(8,128)(2,1)} fusion(bf16[64,128,2,128]{1,0,3,2:T(8,128)(2,1)S(1)} %bitcast.219, bf16[1,128,256]{1,2,0:T(8,128)(2,1)S(1)} %get-tuple-element.39, bf16[1,128,256]{1,2,0:T(8,128)(2,1)S(1)} %get-tuple-element.38), kind=kOutput, calls=%fused_computation.13 | convolution fusion | flops 1076101120 | bytes 8519680 | tf_op jit(solution)/shard_map/ijck,cjb->ibk/dot_general | solution.py:39
  109.8 6.9 %reshape.77 = bf16[64,2,16384]{2,1,0:T(2,128)(2,1)} reshape(bf16[64,256,128]{2,1,0:T(8,128)(2,1)} %fusion.3) | data formatting | bytes 8388608 | tf_op jit(solution)/shard_map/reshape | solution.py:40
  116.7 6.6 %copy.82 = bf16[64,2,16384]{2,0,1:T(8,128)(2,1)} copy(bf16[64,2,16384]{2,1,0:T(2,128)(2,1)} %reshape.77) | data formatting | bytes 8388608 | tf_op jit(solution)/shard_map/reshape | solution.py:40
  123.3 6.2 %pad_maximum_fusion = bf16[2,2,64,16384]{3,2,1,0:T(8,128)(2,1)} fusion(bf16[2,1,64,16384]{3,2,1,0:T(8,128)(2,1)} %bitcast.222, bf16[2,1,64,16384]{3,2,1,0:T(8,128)(2,1)S(1)} %bitcast.220), kind=kLoop, calls=%fused_computation.9 | loop fusion | flops 4194304 | bytes 16777216 | tf_op jit(solution)/shard_map/stack | solution.py:48
  129.5 34.5 %copy.49 = bf16[2,2,64,16384]{2,1,0,3:T(2,128)(2,1)} copy(bf16[2,2,64,16384]{3,2,1,0:T(8,128)(2,1)} %pad_maximum_fusion) | data formatting | bytes 16777216 | tf_op jit(solution)/shard_map/stack | solution.py:48
  164.0 26.7 %reshape.124 = bf16[32,2,65536]{2,1,0:T(2,128)(2,1)} reshape(bf16[16384,2,2,64]{3,2,1,0:T(2,128)(2,1)} %bitcast.211) | data formatting | bytes 16777216
  190.7 5.4 %all-to-all-start = ((bf16[32,2,65536]{2,1,0:T(2,128)(2,1)}), bf16[32,2,65536]{2,1,0:T(2,128)(2,1)}, u32[]{:S(2)}, u32[]{:S(2)}) async-start(bf16[32,2,65536]{2,1,0:T(2,128)(2,1)} %reshape.124), calls=%async_computation | async-start | bytes 16777216 | tf_op jit(solution)/shard_map/all_to_all | solution.py:49
  196.2 5.8 %fusion.56 = (bf16[2,1,2048,512]{3,2,1,0:T(8,128)(2,1)}, bf16[2,1,2048,512]{3,2,1,0:T(8,128)(2,1)}) fusion(bf16[2,2,2048,512]{3,2,1,0:T(8,128)(2,1)} %param.8), kind=kLoop, calls=%fused_computation.112 | loop fusion | bytes 16777216 | tf_op jit(solution)/shard_map/slice | solution.py:53
  202.0 5.0 %gather_fusion.3 = bf16[16,2,128,512]{3,2,1,0:T(8,128)(2,1)} fusion(bf16[2,16,128,512]{3,2,1,0:T(8,128)(2,1)} %bitcast.223, s32[1024]{0:T(1024)S(1)} %pad_clamp_fusion), kind=kCustom, calls=%fused_computation.clone | custom fusion | bytes 8388672 | tf_op jit(solution)/shard_map/jit(_take)/gather | solution.py:54
  207.0 5.0 %gather_fusion.4 = bf16[16,2,128,512]{3,2,1,0:T(8,128)(2,1)} fusion(bf16[2,16,128,512]{3,2,1,0:T(8,128)(2,1)} %bitcast.221, s32[1024]{0:T(1024)S(1)} %pad_clamp_fusion), kind=kCustom, calls=%fused_computation.1.clone | custom fusion | bytes 8388672 | tf_op jit(solution)/shard_map/jit(_take)/gather | solution.py:54
  212.7 6.0 %fusion.5 = (bf16[2,16,128,512]{3,2,1,0:T(8,128)(2,1)}, bf16[2,16,128,512]{3,2,1,0:T(8,128)(2,1)}) fusion(bf16[16,2,128,512]{3,2,1,0:T(8,128)(2,1)} %gather_fusion.3, pred[16]{0:T(512)(128)(4,1)S(1)} %compare_and_fusion, bf16[16,2,128,512]{3,2,1,0:T(8,128)(2,1)} %gather_fusion.4), kind=kLoop, calls=%fused_computation.17 | loop fusion | flops 4194304 | bytes 16777232 | tf_op jit(solution)/shard_map/jit(_take)/select_n | solution.py:54
  220.1 1.5 copy.42
  221.6 1.7 copy.52
  223.3 2.0 gather_fusion.1
  226.0 1.5 copy_convert_fusion.1
  227.6 1.6 copy_convert_fusion
  229.2 75.5 %all-to-all-done = bf16[32,2,65536]{2,1,0:T(2,128)(2,1)} async-done(((bf16[32,2,65536]{2,1,0:T(2,128)(2,1)}), bf16[32,2,65536]{2,1,0:T(2,128)(2,1)}, u32[]{:S(2)}, u32[]{:S(2)}) %all-to-all-start) | async-done | bytes 8388640 | tf_op jit(solution)/shard_map/all_to_all | solution.py:49
  304.7 26.0 %reshape.125 = bf16[16384,2,2,64]{3,2,1,0:T(2,128)(2,1)} reshape(bf16[32,2,65536]{2,1,0:T(2,128)(2,1)} %all-to-all-done) | data formatting | bytes 16777216
  330.7 36.1 %copy.50 = bf16[2,2,32,64,512]{4,3,2,1,0:T(8,128)(2,1)} copy(bf16[2,2,32,64,512]{3,1,0,4,2:T(2,128)(2,1)} %bitcast.212) | data formatting | bytes 16777216 | tf_op jit(solution)/shard_map/all_to_all | solution.py:49
  366.8 4.0 fusion.55
  373.6 1.4 copy-done.2
  380.5 74.2 %psum.7 = f32[2,1,2,16,1]{3,2,0,4,1:T(2,128)S(1)} all-reduce(f32[2,1,2,16,1]{3,2,0,4,1:T(2,128)S(1)} %bitcast.230), channel_id=1, replica_groups=mesh['tm'=4,'op'=32] {'op'}, use_global_device_ids=true, to_apply=%region_4.6 | all-reduce | flops 64 | bytes 512 | tf_op jit(solution)/shard_map/psum | solution.py:74
  (55 shorter events, 19.8 us)
Async XLA Ops:
  6.5 50.8 %all-gather.2.cloned.1.call-start = ((), (), s32[]{:S(2)}) async-start(), calls=%async_computation.1 | async-start | bytes 2162688 | tf_op jit(solution)/shard_map/all_gather | solution.py:20
  93.2 6.6 %copy-start.1 = (bf16[2,8192,128]{2,1,0:T(8,128)(2,1)S(1)}, bf16[2,8192,128]{2,1,0:T(8,128)(2,1)}, u32[]{:S(2)}) copy-start(bf16[2,8192,128]{2,1,0:T(8,128)(2,1)} %reshape_squeeze.19) | copy-start | bytes 12582916
  116.7 6.6 %copy-start.4 = (bf16[64,2,16384]{2,0,1:T(8,128)(2,1)S(1)}, bf16[64,2,16384]{2,0,1:T(8,128)(2,1)}, u32[]{:S(2)}) copy-start(bf16[64,2,16384]{2,0,1:T(8,128)(2,1)} %copy.83) | copy-start | bytes 12582916
  190.7 5.4 %copy-start.8 = (s32[16,1]{0,1:T(1,128)S(1)}, s32[16,1]{0,1:T(1,128)}, u32[]{:S(2)}) copy-start(s32[16,1]{0,1:T(1,128)} %param.10) | copy-start | bytes 196
  190.7 114.0 %all-to-all-start = ((bf16[32,2,65536]{2,1,0:T(2,128)(2,1)}), bf16[32,2,65536]{2,1,0:T(2,128)(2,1)}, u32[]{:S(2)}, u32[]{:S(2)}) async-start(bf16[32,2,65536]{2,1,0:T(2,128)(2,1)} %reshape.124), calls=%async_computation | async-start | bytes 16777216 | tf_op jit(solution)/shard_map/all_to_all | solution.py:49
  207.0 5.0 %copy-start = (s32[16,3]{0,1:T(4,128)S(1)}, s32[16,3]{0,1:T(4,128)}, u32[]{:S(2)}) copy-start(s32[16,3]{0,1:T(4,128)} %param.11) | copy-start | bytes 580
  212.7 6.3 %copy-start.5 = (bf16[2,1,1,512,512]{3,4,2,1,0:T(8,128)(2,1)S(1)}, bf16[2,1,1,512,512]{3,4,2,1,0:T(8,128)(2,1)}, u32[]{:S(2)}) copy-start(bf16[2,1,1,512,512]{3,4,2,1,0:T(8,128)(2,1)} %copy.60) | copy-start | bytes 3145732
  366.8 4.7 %copy-start.3 = (bf16[2,16,128,512]{3,2,1,0:T(8,128)(2,1)S(1)}, bf16[2,16,128,512]{3,2,1,0:T(8,128)(2,1)}, u32[]{:S(2)}) copy-start(bf16[2,16,128,512]{3,2,1,0:T(8,128)(2,1)} %get-tuple-element.48) | copy-start | bytes 12582916
  372.8 2.2 copy-start.2
  376.5 1.6 copy-start.7
  378.0 1.6 copy-start.6
Sparse Core Ops, SparseCore 0:
  9.6 47.6 all-gather.1
where the time goes:
time: 467 us; the launch traced here: 462 us
  local copies, waits for them, and re-layouts  212 us (45%)
  waiting for transfers between devices  110 us (24%)
  blocking collectives  74.2 us (16%)
  matrix products  25.6 us (5%)
  between operations  18.1 us (4%)
  other arithmetic  16.8 us (4%)
  starting transfers between devices  5.43 us (1%)
    all_to_all x1, waiting for transfers between devices, on_device(): lax.all_to_all(stacked, 'op', split_axis=3, concat_axis=2, tiled=True)  75.5 us
    psum x1, blocking collectives, on_device(): totals = lax.psum(partial_sum, 'op')  74.2 us
    unnamed x25, local copies, waits for them, and re-layouts  69.1 us
    all_to_all x1, local copies, waits for them, and re-layouts, on_device(): lax.all_to_all(stacked, 'op', split_axis=3, concat_axis=2, tiled=True)  36.1 us
    all_gather x1, waiting for transfers between devices, on_device(): tau_all = lax.all_gather(peram, 'op', axis=3, tiled=True)  34.7 us
    another operation x1, local copies, waits for them, and re-layouts, on_device(): jnp.stack([sink_side(local, t0, p) for local, t0, p in combos], axis=1)  34.5 us
    reshape x4, local copies, waits for them, and re-layouts, sink_side(): y_both = y_both.astype(jnp.bfloat16).reshape(span, 2, NEV * NEV)  27 us
    dot_general x2, matrix products, sink_side(): jnp.einsum('ijck,cjb->ibk', x_both, second, preferred_element_type=jnp.fl...  14.9 us
  transfers between devices with their start and end apart: 2, of which 2 were waited for; matrix products, arithmetic and copies ran while one was open for 9% of the time, Pallas kernels for 0%

commit v1 on v0

--- a/solution.py
+++ b/solution.py
@@ -17,7 +17,9 @@
 
 
 def on_device(sink_elem, source_elem, peram, pair_list, spin_sets):
-    tau_all = lax.all_gather(peram, "op", axis=3, tiled=True)
+    tau_all = jnp.concatenate(
+        lax.all_to_all(jnp.stack([peram] * lax.axis_size("op")), "op", 0, 0), axis=3
+    )
     position = lax.axis_index("op")
     rows = sink_elem.shape[2]
     local_times = sink_elem.shape[1]

time: 467 us -> 429 us (0.919)
  waiting for transfers between devices: 110 us -> 91 us
  local copies, waits for them, and re-layouts: 212 us -> 197 us
  between operations: 18.1 us -> 4.76 us
  starting transfers between devices: 5.43 us -> 15 us
    all_gather x1 -> x0, waiting for transfers between devices: 34.7 us -> none  [on_device(): tau_all = lax.all_gather(peram, 'op', axis=3, tiled=True)]
    all_to_all x0 -> x1, waiting for transfers between devices: none -> 15.2 us  [on_device(): lax.all_to_all(jnp.stack([peram] * lax.axis_size('op')), 'op', 0, 0)]
    all_to_all x0 -> x1, starting transfers between devices: none -> 9.6 us  [on_device(): lax.all_to_all(jnp.stack([peram] * lax.axis_size('op')), 'op', 0, 0)]
    unnamed x25 -> x22, local copies, waits for them, and re-layouts: 69.1 us -> 60.9 us
    slice x1, local copies, waits for them, and re-layouts: 6.48 us -> 1.16 us  [on_device(): blocks = tau_all[:, combo[0], column_t0].reshape(2, NSPIN, NEV, NSPIN, NEV)]
where the time goes in v1:
time: 429 us; the launch traced here: 425 us
  local copies, waits for them, and re-layouts  197 us (46%)
  waiting for transfers between devices  91 us (21%)
  blocking collectives  75.7 us (18%)
  matrix products  25.6 us (6%)
  other arithmetic  16 us (4%)
  starting transfers between devices  15 us (3%)
  between operations  4.76 us (1%)
    all_to_all x1, waiting for transfers between devices, on_device(): lax.all_to_all(stacked, 'op', split_axis=3, concat_axis=2, tiled=True)  75.8 us
    psum x1, blocking collectives, on_device(): totals = lax.psum(partial_sum, 'op')  75.7 us
    unnamed x22, local copies, waits for them, and re-layouts  60.9 us
    all_to_all x1, local copies, waits for them, and re-layouts, on_device(): lax.all_to_all(stacked, 'op', split_axis=3, concat_axis=2, tiled=True)  36 us
    another operation x1, local copies, waits for them, and re-layouts, on_device(): jnp.stack([sink_side(local, t0, p) for local, t0, p in combos], axis=1)  34.5 us
    reshape x4, local copies, waits for them, and re-layouts, sink_side(): y_both = y_both.astype(jnp.bfloat16).reshape(span, 2, NEV * NEV)  27 us
    all_to_all x1, waiting for transfers between devices, on_device(): lax.all_to_all(jnp.stack([peram] * lax.axis_size('op')), 'op', 0, 0)  15.2 us
    dot_general x2, matrix products, sink_side(): jnp.einsum('ijck,cjb->ibk', x_both, second, preferred_element_type=jnp.fl...  14.9 us
  transfers between devices with their start and end apart: 2, of which 2 were waited for; matrix products, arithmetic and copies ran while one was open for 9% of the time, Pallas kernels for 0%

profile of v1, /device:TPU:1, one launch (start us, length us, event | category | flops | bytes accessed | tf_op | source)
XLA Modules:
  0.0 424.7 jit_solution(8503525131336484363)
XLA Ops:
  0.0 2.5 stack.48
  2.5 9.6 %all-to-all-start = ((bf16[32,2,1,2,16,512]{5,4,3,1,2,0:T(8,128)(2,1)}), bf16[32,2,1,2,16,512]{5,4,3,1,2,0:T(8,128)(2,1)S(1)}, u32[]{:S(2)}, u32[]{:S(2)}) async-start(bf16[32,2,1,2,16,512]{5,4,3,1,2,0:T(8,128)(2,1)} %stack.48), calls=%async_computation | async-start | bytes 4194304 | tf_op jit(solution)/shard_map/all_to_all | solution.py:21
  17.8 7.4 %reshape_squeeze.19 = bf16[2,8192,128]{2,1,0:T(8,128)(2,1)} reshape(bf16[2,1,64,16384]{3,2,1,0:T(8,128)(2,1)} %param.7) | data formatting | bytes 8388608 | tf_op jit(solution)/shard_map/reshape;squeeze | solution.py:38
  25.2 15.2 %all-to-all-done = bf16[32,2,1,2,16,512]{5,4,3,1,2,0:T(8,128)(2,1)S(1)} async-done(((bf16[32,2,1,2,16,512]{5,4,3,1,2,0:T(8,128)(2,1)}), bf16[32,2,1,2,16,512]{5,4,3,1,2,0:T(8,128)(2,1)S(1)}, u32[]{:S(2)}, u32[]{:S(2)}) %all-to-all-start) | async-done | bytes 2097184 | tf_op jit(solution)/shard_map/all_to_all | solution.py:21
  42.4 1.5 copy.61
  43.9 3.5 fusion.15
  47.4 1.2 copy.62
  48.7 7.5 %fusion.2 = bf16[64,256,128]{2,1,0:T(8,128)(2,1)} fusion(bf16[64,128,2,128]{1,0,3,2:T(8,128)(2,1)S(1)} %bitcast.222, bf16[1,128,256]{1,2,0:T(8,128)(2,1)S(1)} %get-tuple-element.35, bf16[1,128,256]{1,2,0:T(8,128)(2,1)S(1)} %get-tuple-element.34), kind=kOutput, calls=%fused_computation.12 | convolution fusion | flops 1076101120 | bytes 8519680 | tf_op jit(solution)/shard_map/ijck,cjb->ibk/dot_general | solution.py:41
  56.1 6.9 %reshape.86 = bf16[64,2,16384]{2,1,0:T(2,128)(2,1)} reshape(bf16[64,256,128]{2,1,0:T(8,128)(2,1)} %fusion.2) | data formatting | bytes 8388608 | tf_op jit(solution)/shard_map/reshape | solution.py:42
  63.0 6.6 %copy.84 = bf16[64,2,16384]{2,0,1:T(8,128)(2,1)} copy(bf16[64,2,16384]{2,1,0:T(2,128)(2,1)} %reshape.86) | data formatting | bytes 8388608 | tf_op jit(solution)/shard_map/reshape | solution.py:42
  69.6 1.3 fusion.14
  70.9 1.2 copy.63
  72.2 7.4 %fusion.3 = bf16[64,256,128]{2,1,0:T(8,128)(2,1)} fusion(bf16[64,128,2,128]{1,0,3,2:T(8,128)(2,1)S(1)} %bitcast.223, bf16[1,128,256]{1,2,0:T(8,128)(2,1)S(1)} %get-tuple-element.39, bf16[1,128,256]{1,2,0:T(8,128)(2,1)S(1)} %get-tuple-element.38), kind=kOutput, calls=%fused_computation.13 | convolution fusion | flops 1076101120 | bytes 8519680 | tf_op jit(solution)/shard_map/ijck,cjb->ibk/dot_general | solution.py:41
  79.6 6.9 %reshape.88 = bf16[64,2,16384]{2,1,0:T(2,128)(2,1)} reshape(bf16[64,256,128]{2,1,0:T(8,128)(2,1)} %fusion.3) | data formatting | bytes 8388608 | tf_op jit(solution)/shard_map/reshape | solution.py:42
  86.5 6.6 %copy.83 = bf16[64,2,16384]{2,0,1:T(8,128)(2,1)} copy(bf16[64,2,16384]{2,1,0:T(2,128)(2,1)} %reshape.88) | data formatting | bytes 8388608 | tf_op jit(solution)/shard_map/reshape | solution.py:42
  93.1 6.2 %pad_maximum_fusion = bf16[2,2,64,16384]{3,2,1,0:T(8,128)(2,1)} fusion(bf16[2,1,64,16384]{3,2,1,0:T(8,128)(2,1)} %bitcast.226, bf16[2,1,64,16384]{3,2,1,0:T(8,128)(2,1)S(1)} %bitcast.224), kind=kLoop, calls=%fused_computation.9 | loop fusion | flops 4194304 | bytes 16777216 | tf_op jit(solution)/shard_map/stack | solution.py:50
  99.3 34.5 %copy.50 = bf16[2,2,64,16384]{2,1,0,3:T(2,128)(2,1)} copy(bf16[2,2,64,16384]{3,2,1,0:T(8,128)(2,1)} %pad_maximum_fusion) | data formatting | bytes 16777216 | tf_op jit(solution)/shard_map/stack | solution.py:50
  133.7 26.7 %reshape.135 = bf16[32,2,65536]{2,1,0:T(2,128)(2,1)} reshape(bf16[16384,2,2,64]{3,2,1,0:T(2,128)(2,1)} %bitcast.215) | data formatting | bytes 16777216
  160.4 5.4 %all-to-all-start.1 = ((bf16[32,2,65536]{2,1,0:T(2,128)(2,1)}), bf16[32,2,65536]{2,1,0:T(2,128)(2,1)}, u32[]{:S(2)}, u32[]{:S(2)}) async-start(bf16[32,2,65536]{2,1,0:T(2,128)(2,1)} %reshape.135), calls=%async_computation.1 | async-start | bytes 16777216 | tf_op jit(solution)/shard_map/all_to_all | solution.py:51
  165.9 5.8 %fusion.56 = (bf16[2,1,2048,512]{3,2,1,0:T(8,128)(2,1)}, bf16[2,1,2048,512]{3,2,1,0:T(8,128)(2,1)}) fusion(bf16[2,2,2048,512]{3,2,1,0:T(8,128)(2,1)} %param.8), kind=kLoop, calls=%fused_computation.112 | loop fusion | bytes 16777216 | tf_op jit(solution)/shard_map/slice | solution.py:55
  171.7 4.9 %gather_fusion.3 = bf16[16,2,128,512]{3,2,1,0:T(8,128)(2,1)} fusion(bf16[2,16,128,512]{3,2,1,0:T(8,128)(2,1)} %bitcast.227, s32[1024]{0:T(1024)S(1)} %pad_clamp_fusion), kind=kCustom, calls=%fused_computation.clone | custom fusion | bytes 8388672 | tf_op jit(solution)/shard_map/jit(_take)/gather | solution.py:56
  176.6 5.0 %gather_fusion.4 = bf16[16,2,128,512]{3,2,1,0:T(8,128)(2,1)} fusion(bf16[2,16,128,512]{3,2,1,0:T(8,128)(2,1)} %bitcast.225, s32[1024]{0:T(1024)S(1)} %pad_clamp_fusion), kind=kCustom, calls=%fused_computation.1.clone | custom fusion | bytes 8388672 | tf_op jit(solution)/shard_map/jit(_take)/gather | solution.py:56
  182.3 5.9 %fusion.5 = (bf16[2,16,128,512]{3,2,1,0:T(8,128)(2,1)}, bf16[2,16,128,512]{3,2,1,0:T(8,128)(2,1)}) fusion(bf16[16,2,128,512]{3,2,1,0:T(8,128)(2,1)} %gather_fusion.3, pred[16]{0:T(512)(128)(4,1)S(1)} %compare_and_fusion, bf16[16,2,128,512]{3,2,1,0:T(8,128)(2,1)} %gather_fusion.4), kind=kLoop, calls=%fused_computation.17 | loop fusion | flops 4194304 | bytes 16777232 | tf_op jit(solution)/shard_map/jit(_take)/select_n | solution.py:56
  189.6 1.8 copy.43
  193.7 1.6 copy_convert_fusion.1
  195.2 1.6 copy_convert_fusion
  196.8 75.8 %all-to-all-done.1 = bf16[32,2,65536]{2,1,0:T(2,128)(2,1)} async-done(((bf16[32,2,65536]{2,1,0:T(2,128)(2,1)}), bf16[32,2,65536]{2,1,0:T(2,128)(2,1)}, u32[]{:S(2)}, u32[]{:S(2)}) %all-to-all-start.1) | async-done | bytes 8388640 | tf_op jit(solution)/shard_map/all_to_all | solution.py:51
  272.6 26.0 %reshape.136 = bf16[16384,2,2,64]{3,2,1,0:T(2,128)(2,1)} reshape(bf16[32,2,65536]{2,1,0:T(2,128)(2,1)} %all-to-all-done.1) | data formatting | bytes 16777216
  298.7 36.0 %copy.51 = bf16[2,2,32,64,512]{4,3,2,1,0:T(8,128)(2,1)} copy(bf16[2,2,32,64,512]{3,1,0,4,2:T(2,128)(2,1)} %bitcast.216) | data formatting | bytes 16777216 | tf_op jit(solution)/shard_map/all_to_all | solution.py:51
  334.7 4.0 fusion.55
  341.5 1.4 copy-done.2
  348.4 75.7 %psum.7 = f32[2,1,2,16,1]{3,2,0,4,1:T(2,128)S(1)} all-reduce(f32[2,1,2,16,1]{3,2,0,4,1:T(2,128)S(1)} %bitcast.236), channel_id=1, replica_groups=mesh['tm'=4,'op'=32] {'op'}, use_global_device_ids=true, to_apply=%region_4.6 | all-reduce | flops 64 | bytes 512 | tf_op jit(solution)/shard_map/psum | solution.py:76
  (53 shorter events, 16.6 us)
Async XLA Ops:
  0.0 12.1 %copy-start.7 = (s32[16,1]{0,1:T(1,128)S(1)}, s32[16,1]{0,1:T(1,128)}, u32[]{:S(2)}) copy-start(s32[16,1]{0,1:T(1,128)} %param.10) | copy-start | bytes 196
  0.0 14.6 %copy-start = (s32[16,3]{0,1:T(4,128)S(1)}, s32[16,3]{0,1:T(4,128)}, u32[]{:S(2)}) copy-start(s32[16,3]{0,1:T(4,128)} %param.11) | copy-start | bytes 580
  2.5 37.9 %all-to-all-start = ((bf16[32,2,1,2,16,512]{5,4,3,1,2,0:T(8,128)(2,1)}), bf16[32,2,1,2,16,512]{5,4,3,1,2,0:T(8,128)(2,1)S(1)}, u32[]{:S(2)}, u32[]{:S(2)}) async-start(bf16[32,2,1,2,16,512]{5,4,3,1,2,0:T(8,128)(2,1)} %stack.48), calls=%async_computation | async-start | bytes 4194304 | tf_op jit(solution)/shard_map/all_to_all | solution.py:21
  63.0 6.6 %copy-start.1 = (bf16[2,8192,128]{2,1,0:T(8,128)(2,1)S(1)}, bf16[2,8192,128]{2,1,0:T(8,128)(2,1)}, u32[]{:S(2)}) copy-start(bf16[2,8192,128]{2,1,0:T(8,128)(2,1)} %reshape_squeeze.19) | copy-start | bytes 12582916
  86.5 6.6 %copy-start.4 = (bf16[64,2,16384]{2,0,1:T(8,128)(2,1)S(1)}, bf16[64,2,16384]{2,0,1:T(8,128)(2,1)}, u32[]{:S(2)}) copy-start(bf16[64,2,16384]{2,0,1:T(8,128)(2,1)} %copy.84) | copy-start | bytes 12582916
  160.4 112.2 %all-to-all-start.1 = ((bf16[32,2,65536]{2,1,0:T(2,128)(2,1)}), bf16[32,2,65536]{2,1,0:T(2,128)(2,1)}, u32[]{:S(2)}, u32[]{:S(2)}) async-start(bf16[32,2,65536]{2,1,0:T(2,128)(2,1)} %reshape.135), calls=%async_computation.1 | async-start | bytes 16777216 | tf_op jit(solution)/shard_map/all_to_all | solution.py:51
  334.7 4.7 %copy-start.3 = (bf16[2,16,128,512]{3,2,1,0:T(8,128)(2,1)S(1)}, bf16[2,16,128,512]{3,2,1,0:T(8,128)(2,1)}, u32[]{:S(2)}) copy-start(bf16[2,16,128,512]{3,2,1,0:T(8,128)(2,1)} %get-tuple-element.48) | copy-start | bytes 12582916
  340.8 2.2 copy-start.2
  344.4 1.6 copy-start.6
  346.0 1.6 copy-start.5
